TPU v7x, 32 devices: a whole 2x2x4 slice. The times are simulated.
32 devices in a mesh: fsdp: 8 (over z, y), tp: 4 (over x, core).
Axes of the slice: x: 2, y: 2, z: 4, core: 2. Of those that a mesh axis runs over, the one named last changes fastest.
Arguments:
- grads: bfloat16 [8, 2, 4096, 2048], P('fsdp', None, 'tp'), may hold values from -144 to 144
- master: float32 [4096, 2048], P('tp', 'fsdp'), may hold values from -0.3125 to 0.3125
- moment: float32 [4096, 2048], P('tp', 'fsdp'), may hold values from -1.5 to 1.5
- second: float32 [4096, 2048], P('tp', 'fsdp'), may hold values from 0.02 to 0.3
- stats: float32 [4, 1024, 1024], P('tp', 'fsdp'), may hold values from -0.05 to 0.35
- basis: float32 [4, 1024, 1024], P('tp', 'fsdp'), may hold values from -0.5 to 1.5
Outputs:
- weights: bfloat16 [4096, 2048], P('tp')
- master_new: float32 [4096, 2048], P('tp', 'fsdp')
- moment_new: float32 [4096, 2048], P('tp', 'fsdp')
- second_new: float32 [4096, 2048], P('tp', 'fsdp')
- stats_new: float32 [4, 1024, 1024], P('tp', 'fsdp')
- basis_new: float32 [4, 1024, 1024], P('tp', 'fsdp')
All inputs are finite; a program needn't handle non-finite values.
Results may differ from a plain program's by a relative error of at most 0.007.
Values may be sent and summed in bfloat16 or wider, within the bound.
A program may use at most 128 MiB of HBM per device.

v0:
```python
import jax
import jax.numpy as jnp
from jax import lax
from jax.sharding import PartitionSpec as P

D = 4096
KVW = 2048
NSK = 2
poly_first = 3.4445
poly_second = -4.775
poly_third = 2.0315


def gram_of(current):
    local_gram = jnp.dot(current.T, current, precision=lax.Precision.HIGHEST)
    return lax.psum(local_gram.astype(jnp.bfloat16), "fsdp").astype(jnp.float32)


def body(grads, master, moment, second, stats, basis):
    high = lax.Precision.HIGHEST
    local = jnp.sum(grads.astype(jnp.float32), axis=(0, 1))
    summed = lax.psum_scatter(local, "fsdp", scatter_dimension=1, tiled=True)
    squares = lax.psum(jnp.sum(summed * summed), ("fsdp", "tp"))
    clipped = summed * jnp.minimum(1.0, jnp.sqrt(float(D * KVW) / (squares + 1e-06)))
    own_rows = basis[0]
    stat_rows = stats[0]
    whole = lax.all_gather(own_rows, "fsdp", axis=0, tiled=True)
    rotated = jnp.dot(whole.T, clipped, precision=high)
    moment_new = 0.9 * moment + 0.1 * rotated
    second_new = 0.95 * second + 0.05 * rotated * rotated
    update = moment_new / (jnp.sqrt(second_new) + 1e-08)
    delta = jnp.dot(whole, update, precision=high)
    master_new = master - 0.01 * (delta + 0.1 * master)
    weights = lax.all_gather(master_new.astype(jnp.bfloat16), "fsdp", axis=1, tiled=True)
    outer = lax.psum_scatter(
        jnp.dot(clipped, clipped.T, precision=high).astype(jnp.bfloat16),
        "fsdp",
        scatter_dimension=0,
        tiled=True,
    ).astype(jnp.float32)
    stats_new = 0.9 * stat_rows + 0.1 / KVW * outer
    power = jnp.dot(stats_new, whole, precision=high)
    total_sq = lax.psum(jnp.sum(power * power), "fsdp")
    current = power / jnp.sqrt(total_sq + 1e-06)
    first_gram = gram_of(current)
    for step in range(NSK):
        gram = first_gram if step == 0 else gram_of(current)
        product = jnp.dot(current, gram, precision=high)
        second_term = jnp.dot(product, gram, precision=high)
        current = poly_first * current + poly_second * product + poly_third * second_term
    return (weights, master_new, moment_new, second_new, stats_new[None], current[None])


def solution(mesh):
    in_specs = (
        P("fsdp", None, "tp", None),
        P("tp", "fsdp"),
        P("tp", "fsdp"),
        P("tp", "fsdp"),
        P("tp", "fsdp", None),
        P("tp", "fsdp", None),
    )
    out_specs = (
        P("tp", None),
        P("tp", "fsdp"),
        P("tp", "fsdp"),
        P("tp", "fsdp"),
        P("tp", "fsdp", None),
        P("tp", "fsdp", None),
    )
    return jax.shard_map(body, mesh=mesh, in_specs=in_specs, out_specs=out_specs, check_vma=False)
```

profile of v0, /device:TPU:0, one launch (start us, length us, event | category | flops | bytes accessed | tf_op | source)
XLA Modules:
  0.0 637.1 jit_solution(12777365153382909776)
XLA Ops:
  7.2 9.6 %convert_reduce_fusion = f32[1024,2048]{1,0:T(8,128)} fusion(bf16[1,2,1024,2048]{3,2,1,0:T(8,128)(2,1)} %param.6), kind=kLoop, calls=%fused_computation | loop fusion | flops 6291456 | bytes 16777216 | tf_op jit(solution)/shard_map/reduce_sum | solution.py:21
  16.9 0.7 all-gather.6.cloned.1.call-update
  17.6 151.5 %reduce-scatter.3.cloned.1.call-done = f32[1024,256]{1,0:T(8,128)} async-done(((f32[1024,2048]{1,0:T(8,128)}), f32[1024,256]{1,0:T(8,128)}) %reduce-scatter.3.cloned.1.call-update) | async-done | bytes 1048592 | tf_op jit(solution)/shard_map/reduce_scatter | solution.py:22
  169.1 2.1 multiply_reduce_fusion
  171.2 40.6 %psum.28 = f32[]{:T(128)} all-reduce(f32[]{:T(128)} %multiply_reduce_fusion), channel_id=1, replica_groups=mesh['fsdp'=8,'tp'=4] {'fsdp','tp'}, use_global_device_ids=true, to_apply=%region_3.0 | all-reduce | flops 1 | bytes 8 | tf_op jit(solution)/shard_map/psum | solution.py:23
  212.6 6.4 %convolution_convert_fusion.2 = bf16[1024,1024]{1,0:T(8,128)(2,1)} fusion(f32[1024,256]{1,0:T(8,128)} %reduce-scatter.3.cloned.1.call-done, f32[]{:T(128)S(6)} %min_shard_map.3), kind=kOutput, calls=%fused_computation.9 | convolution fusion | flops 3222536192 | bytes 3145732 | tf_op jit(solution)/shard_map/dot_general | solution.py:36
  219.0 0.0 all-reduce.3.cloned.1.call-start
  219.1 26.4 %all-gather.6.cloned.1.call-done = f32[1,1024,1024]{2,1,0:T(8,128)} async-done(((f32[1,128,1024]{2,1,0:T(8,128)}), f32[1,1024,1024]{2,1,0:T(8,128)}) %all-gather.6.cloned.1.call-update) | async-done | bytes 4194320 | tf_op jit(solution)/shard_map/all_gather | solution.py:27
  245.4 70.4 %reduce-scatter.5.cloned.1.call-done = bf16[128,1024]{1,0:T(8,128)(2,1)} async-done(((bf16[1024,1024]{1,0:T(8,128)(2,1)}), bf16[128,1024]{1,0:T(8,128)(2,1)}) %reduce-scatter.5.cloned.1.call-update) | async-done | bytes 262160 | tf_op jit(solution)/shard_map/reduce_scatter | solution.py:35
  315.8 5.3 multiply_reduce_fusion.1
  321.2 19.9 %psum.29 = f32[]{:T(128)} all-reduce(f32[]{:T(128)} %get-tuple-element.22), channel_id=1, replica_groups=mesh['fsdp'=8,'tp'=4] {'fsdp'}, use_global_device_ids=true, to_apply=%region_6.0 | all-reduce | flops 1 | bytes 8 | tf_op jit(solution)/shard_map/psum | solution.py:43
  341.8 4.7 convolution_convert_fusion.1
  346.5 0.0 all-gather.4.cloned.1.call-start
  346.6 1.3 copy.20
  347.9 2.5 copy.21
  350.4 2.5 copy.23
  352.9 6.7 %fusion.24 = (f32[1024,256]{0,1:T(8,128)S(1)}, f32[1024,256]{0,1:T(8,128)S(1)}) fusion(f32[1024,256]{0,1:T(8,128)} %copy.21, f32[1024,256]{0,1:T(8,128)} %copy.20, f32[1,1024,1024]{2,1,0:T(8,128)} %all-gather.6.cloned.1.call-done, f32[1024,256]{1,0:T(8,128)S(1)} %copy-done.1, f32[]{:T(128)S(6)} %min_shard_map.3), kind=kOutput, calls=%fused_computation.21 | convolution fusion | flops 3223322624 | bytes 9437188 | tf_op jit(solution)/shard_map/dot_general | solution.py:28
  359.6 5.3 fusion.40
  364.9 0.3 all-reduce.5.cloned.1.call-start
  365.2 80.5 %all-reduce.3.cloned.1.call-done = bf16[1024,1024]{1,0:T(8,128)(2,1)} async-done(((bf16[1024,1024]{1,0:T(8,128)(2,1)}), bf16[1024,1024]{1,0:T(8,128)(2,1)}) %all-reduce.3.cloned.1.call-update) | async-done | bytes 2097168 | tf_op jit(solution)/shard_map/psum | solution.py:16
  445.7 2.6 fusion.39
  448.4 2.6 fusion.23
  451.0 4.7 convolution_convert_fusion
  455.8 1.3 copy.26
  457.1 1.3 copy.27
  458.4 2.5 copy.25
  460.9 0.9 fusion.33
  461.8 59.9 %all-gather.4.cloned.1.call-done = bf16[1024,2048]{0,1:T(8,128)(2,1)} async-done(((bf16[1024,256]{0,1:T(8,128)(2,1)}), bf16[1024,2048]{0,1:T(8,128)(2,1)}) %all-gather.4.cloned.1.call-update) | async-done | bytes 4194320 | tf_op jit(solution)/shard_map/all_gather | solution.py:34
  521.7 6.4 %copy.24 = bf16[1024,2048]{1,0:T(8,128)(2,1)} copy(bf16[1024,2048]{0,1:T(8,128)(2,1)} %all-gather.4.cloned.1.call-done) | data formatting | bytes 8388608
  528.1 97.6 %all-reduce.5.cloned.1.call-done = bf16[1024,1024]{1,0:T(8,128)(2,1)} async-done(((bf16[1024,1024]{1,0:T(8,128)(2,1)}), bf16[1024,1024]{1,0:T(8,128)(2,1)}) %all-reduce.5.cloned.1.call-update) | async-done | bytes 2097168 | tf_op jit(solution)/shard_map/psum | solution.py:16
  625.7 2.8 fusion.41
  628.4 1.9 fusion.22
  (28 shorter events, 0.2 us)
Async XLA Ops:
  7.2 161.9 %reduce-scatter.3.cloned.1.call-start = ((), (), s32[]{:S(2)}) async-start(), calls=%async_computation.2 | async-start | bytes 9437184 | tf_op jit(solution)/shard_map/reduce_scatter | solution.py:22
  16.8 299.0 %copy-start.4 = (f32[1,128,1024]{2,1,0:T(8,128)S(1)}, f32[1,128,1024]{2,1,0:T(8,128)}, u32[]{:S(2)}) copy-start(f32[1,128,1024]{2,1,0:T(8,128)} %param.10) | copy-start | bytes 1572868
  16.8 228.6 %all-gather.6.cloned.1.call-start = ((), (), s32[]{:S(2)}) async-start(), calls=%async_computation.7 | async-start | bytes 4718592 | tf_op jit(solution)/shard_map/all_gather | solution.py:27
  17.6 298.2 %reduce-scatter.5.cloned.1.call-start = ((), (), s32[]{:S(2)}) async-start(), calls=%async_computation.4 | async-start | bytes 2359296 | tf_op jit(solution)/shard_map/reduce_scatter | solution.py:35
  219.0 127.5 %copy-start.9 = (f32[1024,256]{1,0:T(8,128)S(1)}, f32[1024,256]{1,0:T(8,128)}, u32[]{:S(2)}) copy-start(f32[1024,256]{1,0:T(8,128)} %param.8) | copy-start | bytes 3145732
  219.0 226.7 %all-reduce.3.cloned.1.call-start = ((), (), s32[]{:S(2)}) async-start(), calls=%async_computation.5 | async-start | bytes 4194304 | tf_op jit(solution)/shard_map/psum | solution.py:16
  321.2 29.2 %copy-start.6 = (f32[128,1024]{1,0:T(8,128)}, f32[128,1024]{1,0:T(8,128)S(1)}, u32[]{:S(2)}) copy-start(f32[128,1024]{1,0:T(8,128)S(1)} %get-tuple-element.23) | copy-start | bytes 1572868
  346.5 6.5 %copy-start.1 = (f32[1024,256]{1,0:T(8,128)S(1)}, f32[1024,256]{1,0:T(8,128)}, u32[]{:S(2)}) copy-start(f32[1024,256]{1,0:T(8,128)} %reduce-scatter.3.cloned.1.call-done) | copy-start | bytes 3145732
  346.5 175.2 %all-gather.4.cloned.1.call-start = ((), (), s32[]{:S(2)}) async-start(), calls=%async_computation.3 | async-start | bytes 4718592 | tf_op jit(solution)/shard_map/all_gather | solution.py:34
  352.9 6.7 %copy-start = (f32[1,1024,1024]{2,1,0:T(8,128)S(1)}, f32[1,1024,1024]{2,1,0:T(8,128)}, u32[]{:S(2)}) copy-start(f32[1,1024,1024]{2,1,0:T(8,128)} %all-gather.6.cloned.1.call-done) | copy-start | bytes 12582916
  352.9 6.7 %copy-start.3 = (f32[1024,256]{0,1:T(8,128)S(1)}, f32[1024,256]{0,1:T(8,128)}, u32[]{:S(2)}) copy-start(f32[1024,256]{0,1:T(8,128)} %copy.23) | copy-start | bytes 3145732
  359.6 86.1 %copy-start.7 = (f32[128,1024]{1,0:T(8,128)S(1)}, f32[128,1024]{1,0:T(8,128)}, u32[]{:S(2)}) copy-start(f32[128,1024]{1,0:T(8,128)} %copy-done.6) | copy-start | bytes 1572868
  364.9 260.7 %all-reduce.5.cloned.1.call-start = ((), (), s32[]{:S(2)}) async-start(), calls=%async_computation.6 | async-start | bytes 4194304 | tf_op jit(solution)/shard_map/psum | solution.py:16
  455.7 5.2 copy-start.5
  455.7 5.2 copy-start.8
  625.7 2.8 copy-start.2
Sparse Core Ops, SparseCore 0:
  16.9 152.0 reduce-scatter.2
  171.4 73.9 all-gather.5
  250.0 65.8 reduce-scatter.4
  346.6 99.0 all-reduce.2
  448.5 73.1 all-gather.3
  525.6 100.0 all-reduce.4
where the time goes:
time: 638 us; the launch traced here: 637 us
  waiting for transfers between devices  487 us (76%)
  blocking collectives  60.5 us (9%)
  matrix products  43 us (7%)
  local copies, waits for them, and re-layouts  18 us (3%)
  between operations  15.6 us (2%)
  other arithmetic  12.6 us (2%)
    psum x2, waiting for transfers between devices, gram_of(): return lax.psum(local_gram.astype(jnp.bfloat16), 'fsdp').astype(jnp.float32)  178 us
    reduce_scatter x1, waiting for transfers between devices, body(): summed = lax.psum_scatter(local, 'fsdp', scatter_dimension=1, tiled=True)  151 us
    reduce_scatter x1, waiting for transfers between devices, body(): lax.psum_scatter(jnp.dot(clipped, clipped.T, precision=high).astype(jnp.b...  70.4 us
    all_gather x1, waiting for transfers between devices, body(): lax.all_gather(master_new.astype(jnp.bfloat16), 'fsdp', axis=1, tiled=True)  59.9 us
    psum x1, blocking collectives, body(): squares = lax.psum(jnp.sum(summed * summed), ('fsdp', 'tp'))  40.6 us
    all_gather x1, waiting for transfers between devices, body(): whole = lax.all_gather(own_rows, 'fsdp', axis=0, tiled=True)  26.4 us
    psum x1, blocking collectives, body(): total_sq = lax.psum(jnp.sum(power * power), 'fsdp')  19.9 us
    unnamed x27, local copies, waits for them, and re-layouts  18 us
  transfers between devices with their start and end apart: 6, of which 6 were waited for; matrix products, arithmetic and copies ran while one was open for 8% of the time, Pallas kernels for 0%

commit v1 on v0

--- a/solution.py
+++ b/solution.py
@@ -2,6 +2,7 @@
 import jax.numpy as jnp
 from jax import lax
 from jax.sharding import PartitionSpec as P
+from jax.lax import all_gather
 
 D = 4096
 KVW = 2048
@@ -13,7 +14,9 @@
 
 def gram_of(current):
     local_gram = jnp.dot(current.T, current, precision=lax.Precision.HIGHEST)
-    return lax.psum(local_gram.astype(jnp.bfloat16), "fsdp").astype(jnp.float32)
+    return jnp.sum(all_gather(local_gram.astype(jnp.bfloat16), axis_name="fsdp"), axis=0).astype(
+        jnp.float32
+    )
 
 
 def body(grads, master, moment, second, stats, basis):

time: 638 us -> 894 us (1.40)
  waiting for transfers between devices: 487 us -> 724 us
  other arithmetic: 12.6 us -> 32.9 us
    all_gather x0 -> x2, waiting for transfers between devices: none -> 427 us  [gram_of(): all_gather(local_gram.astype(jnp.bfloat16), axis_name='fsdp')]
    psum x2 -> x0, waiting for transfers between devices: 178 us -> none  [gram_of(): return lax.psum(local_gram.astype(jnp.bfloat16), 'fsdp').astype(jnp.float32)]
    reduce_sum x0 -> x2, other arithmetic: none -> 20.4 us  [gram_of(): jnp.sum(all_gather(local_gram.astype(jnp.bfloat16), axis_name='fsdp'), ax...]
    all_gather x1, waiting for transfers between devices: 59.9 us -> 47.3 us  [body(): lax.all_gather(master_new.astype(jnp.bfloat16), 'fsdp', axis=1, tiled=True)]
    unnamed x27 -> x25, local copies, waits for them, and re-layouts: 18 us -> 18.2 us
  transfers between devices with their start and end apart: 6 -> 6, of which waited for: 6 -> 6; matrix products, arithmetic and copies ran while one was open for 8% -> 7% of each run, Pallas kernels for 0% -> 0%
where the time goes in v1:
time: 894 us
  waiting for transfers between devices  724 us (81%)
  blocking collectives  60.6 us (7%)
  matrix products  42.2 us (5%)
  other arithmetic  32.9 us (4%)
  local copies, waits for them, and re-layouts  18.2 us (2%)
  between operations  15.6 us (2%)
    all_gather x2, waiting for transfers between devices, gram_of(): all_gather(local_gram.astype(jnp.bfloat16), axis_name='fsdp')  427 us
    reduce_scatter x1, waiting for transfers between devices, body(): summed = lax.psum_scatter(local, 'fsdp', scatter_dimension=1, tiled=True)  151 us
    reduce_scatter x1, waiting for transfers between devices, body(): lax.psum_scatter(jnp.dot(clipped, clipped.T, precision=high).astype(jnp.b...  70.7 us
    all_gather x1, waiting for transfers between devices, body(): lax.all_gather(master_new.astype(jnp.bfloat16), 'fsdp', axis=1, tiled=True)  47.3 us
    psum x1, blocking collectives, body(): squares = lax.psum(jnp.sum(summed * summed), ('fsdp', 'tp'))  40.6 us
    all_gather x1, waiting for transfers between devices, body(): whole = lax.all_gather(own_rows, 'fsdp', axis=0, tiled=True)  26.5 us
    reduce_sum x2, other arithmetic, gram_of(): jnp.sum(all_gather(local_gram.astype(jnp.bfloat16), axis_name='fsdp'), ax...  20.4 us
    psum x1, blocking collectives, body(): total_sq = lax.psum(jnp.sum(power * power), 'fsdp')  20 us
  transfers between devices with their start and end apart: 6, of which 6 were waited for; matrix products, arithmetic and copies ran while one was open for 7% of the time, Pallas kernels for 0%

profile of v1, /device:TPU:0, one launch (start us, length us, event | category | flops | bytes accessed | tf_op | source)
XLA Modules:
  0.0 893.6 jit_solution(2117042240737282096)
XLA Ops:
  7.2 9.6 %convert_reduce_fusion = f32[1024,2048]{1,0:T(8,128)} fusion(bf16[1,2,1024,2048]{3,2,1,0:T(8,128)(2,1)} %param.6), kind=kLoop, calls=%fused_computation | loop fusion | flops 6291456 | bytes 16777216 | tf_op jit(solution)/shard_map/reduce_sum | solution.py:24
  16.9 0.7 all-gather.10.cloned.1.call-update
  17.6 151.5 %reduce-scatter.3.cloned.1.call-done = f32[1024,256]{1,0:T(8,128)} async-done(((f32[1024,2048]{1,0:T(8,128)}), f32[1024,256]{1,0:T(8,128)}) %reduce-scatter.3.cloned.1.call-update) | async-done | bytes 1048592 | tf_op jit(solution)/shard_map/reduce_scatter | solution.py:25
  169.1 2.1 multiply_reduce_fusion
  171.2 40.6 %psum.14 = f32[]{:T(128)} all-reduce(f32[]{:T(128)} %multiply_reduce_fusion), channel_id=1, replica_groups=mesh['fsdp'=8,'tp'=4] {'fsdp','tp'}, use_global_device_ids=true, to_apply=%region_3.0 | all-reduce | flops 1 | bytes 8 | tf_op jit(solution)/shard_map/psum | solution.py:26
  212.5 6.4 convolution_convert_fusion.2
  219.0 26.5 %all-gather.10.cloned.1.call-done = f32[1,1024,1024]{2,1,0:T(8,128)} async-done(((f32[1,128,1024]{2,1,0:T(8,128)}), f32[1,1024,1024]{2,1,0:T(8,128)}) %all-gather.10.cloned.1.call-update) | async-done | bytes 4194320 | tf_op jit(solution)/shard_map/all_gather | solution.py:30
  245.4 70.7 %reduce-scatter.5.cloned.1.call-done = bf16[128,1024]{1,0:T(8,128)(2,1)} async-done(((bf16[1024,1024]{1,0:T(8,128)(2,1)}), bf16[128,1024]{1,0:T(8,128)(2,1)}) %reduce-scatter.5.cloned.1.call-update) | async-done | bytes 262160 | tf_op jit(solution)/shard_map/reduce_scatter | solution.py:38
  316.1 5.3 multiply_reduce_fusion.1
  321.5 20.0 %psum.15 = f32[]{:T(128)} all-reduce(f32[]{:T(128)} %get-tuple-element.22), channel_id=1, replica_groups=mesh['fsdp'=8,'tp'=4] {'fsdp'}, use_global_device_ids=true, to_apply=%region_6.0 | all-reduce | flops 1 | bytes 8 | tf_op jit(solution)/shard_map/psum | solution.py:46
  342.1 4.7 convolution_convert_fusion.1
  346.9 1.3 copy.20
  348.2 2.5 copy.21
  350.8 2.7 copy.23
  353.5 7.5 fusion.24
  361.0 5.3 fusion.40
  366.3 0.3 all-gather.14.cloned.1.call-start
  366.6 205.3 %all-gather.12.cloned.1.call-done = bf16[8192,1024]{1,0:T(8,128)(2,1)} async-done(((bf16[1024,1024]{1,0:T(8,128)(2,1)}), bf16[8192,1024]{1,0:T(8,128)(2,1)}) %all-gather.12.cloned.1.call-update) | async-done | bytes 16777232 | tf_op jit(solution)/shard_map/all_gather | solution.py:17
  571.9 10.9 %reduce_sum.54 = bf16[1024,1024]{1,0:T(8,128)(2,1)} reduce(bf16[8,1024,1024]{2,1,0:T(8,128)(2,1)} %bitcast.55, bf16[]{:T(256)} %constant.14.clone.1), dimensions={0}, to_apply=%region_7.0 | reduce | flops 7340032 | bytes 18874370 | tf_op jit(solution)/shard_map/reduce_sum | solution.py:17
  582.8 2.6 fusion.39
  585.4 2.7 fusion.23
  588.1 4.8 convolution_convert_fusion
  592.9 1.3 copy.26
  594.2 1.3 copy.27
  595.5 2.5 copy.25
  598.1 0.9 fusion.33
  598.9 47.3 %all-gather.8.cloned.1.call-done = bf16[1024,2048]{0,1:T(8,128)(2,1)} async-done(((bf16[1024,256]{0,1:T(8,128)(2,1)}), bf16[1024,2048]{0,1:T(8,128)(2,1)}) %all-gather.8.cloned.1.call-update) | async-done | bytes 4194320 | tf_op jit(solution)/shard_map/all_gather | solution.py:37
  646.3 6.4 copy.24
  652.7 221.7 %all-gather.14.cloned.1.call-done = bf16[8192,1024]{1,0:T(8,128)(2,1)} async-done(((bf16[1024,1024]{1,0:T(8,128)(2,1)}), bf16[8192,1024]{1,0:T(8,128)(2,1)}) %all-gather.14.cloned.1.call-update) | async-done | bytes 16777232 | tf_op jit(solution)/shard_map/all_gather | solution.py:17
  874.4 9.5 %reduce_sum.55 = bf16[1024,1024]{1,0:T(8,128)(2,1)S(1)} reduce(bf16[8,1024,1024]{2,1,0:T(8,128)(2,1)} %bitcast.56, bf16[]{:T(256)} %constant.14.clone.1), dimensions={0}, to_apply=%region_8.0 | reduce | flops 7340032 | bytes 18874370 | tf_op jit(solution)/shard_map/reduce_sum | solution.py:17
  883.8 1.0 fusion.41
  884.9 1.9 fusion.22
  (28 shorter events, 0.3 us)
Async XLA Ops:
  7.2 161.9 %reduce-scatter.3.cloned.1.call-start = ((), (), s32[]{:S(2)}) async-start(), calls=%async_computation.2 | async-start | bytes 9437184 | tf_op jit(solution)/shard_map/reduce_scatter | solution.py:25
  16.8 299.3 %copy-start.3 = (f32[1,128,1024]{2,1,0:T(8,128)S(1)}, f32[1,128,1024]{2,1,0:T(8,128)}, u32[]{:S(2)}) copy-start(f32[1,128,1024]{2,1,0:T(8,128)} %param.10) | copy-start | bytes 1572868
  16.8 228.6 %all-gather.10.cloned.1.call-start = ((), (), s32[]{:S(2)}) async-start(), calls=%async_computation.5 | async-start | bytes 4718592 | tf_op jit(solution)/shard_map/all_gather | solution.py:30
  17.6 298.6 %reduce-scatter.5.cloned.1.call-start = ((), (), s32[]{:S(2)}) async-start(), calls=%async_computation.4 | async-start | bytes 2359296 | tf_op jit(solution)/shard_map/reduce_scatter | solution.py:38
  218.9 128.0 %copy-start.8 = (f32[1024,256]{1,0:T(8,128)S(1)}, f32[1024,256]{1,0:T(8,128)}, u32[]{:S(2)}) copy-start(f32[1024,256]{1,0:T(8,128)} %param.8) | copy-start | bytes 3145732
  218.9 352.9 %all-gather.12.cloned.1.call-start = ((), (), s32[]{:S(2)}) async-start(), calls=%async_computation.6 | async-start | bytes 18874368 | tf_op jit(solution)/shard_map/all_gather | solution.py:17
  321.5 29.3 %copy-start.5 = (f32[128,1024]{1,0:T(8,128)}, f32[128,1024]{1,0:T(8,128)S(1)}, u32[]{:S(2)}) copy-start(f32[128,1024]{1,0:T(8,128)S(1)} %get-tuple-element.23) | copy-start | bytes 1572868
  346.8 6.6 copy-start.1
  346.9 299.4 %all-gather.8.cloned.1.call-start = ((), (), s32[]{:S(2)}) async-start(), calls=%async_computation.3 | async-start | bytes 4718592 | tf_op jit(solution)/shard_map/all_gather | solution.py:37
  353.5 7.5 copy-start
  353.5 7.6 copy-start.2
  366.3 508.0 %all-gather.14.cloned.1.call-start = ((), (), s32[]{:S(2)}) async-start(), calls=%async_computation.7 | async-start | bytes 18874368 | tf_op jit(solution)/shard_map/all_gather | solution.py:17
  571.9 10.9 %copy-start.6 = (f32[128,1024]{1,0:T(8,128)S(1)}, f32[128,1024]{1,0:T(8,128)}, u32[]{:S(2)}) copy-start(f32[128,1024]{1,0:T(8,128)} %copy-done.5) | copy-start | bytes 1572868
  592.9 5.2 copy-start.4
  592.9 5.2 copy-start.7
Sparse Core Ops, SparseCore 0:
  16.9 152.0 reduce-scatter.2
  171.4 73.9 all-gather.9
  250.0 66.1 reduce-scatter.4
  347.0 224.8 all-gather.11
  574.6 71.5 all-gather.7
  648.5 225.8 all-gather.13
